TPU v7x, 128 devices: a whole 4x4x4 slice. The times are simulated.
128 devices in a mesh: ctx: 32 (over z, x, core), head: 4 (over y).
Axes of the slice: x: 4, y: 4, z: 4, core: 2. Of those that a mesh axis runs over, the one named last changes fastest.
Arguments:
- queries: bfloat16 [16384, 2048], P('ctx', 'head'), may hold values from -6 to 6
- key_rows: bfloat16 [16384, 2048], P('ctx', 'head'), may hold values from -6 to 6
- value_rows: bfloat16 [16384, 2048], P('ctx', 'head'), may hold values from -6 to 6
- targets: bfloat16 [16384, 512], P('ctx'), may hold values from -2.5 to 2.5
- readout: bfloat16 [512, 4096], P(None, 'head'), may hold values from -0.25 to 0.25
- retain: float32 [32, 16], P('ctx', 'head'), may hold values from 0.3 to 1
- learn_rate: float32 [32, 16], P('ctx', 'head'), may hold values from 0.01 to 0.1
- allowed: int32 [32, 2], replicated, may hold values 0 or 1
- positions: int32 [32, 128], P('ctx'), may hold values from 0 to 511, as said below
- grad_out: bfloat16 [16384, 2048], P('ctx', 'head'), may hold values from -6 to 6
Outputs:
- grad_queries: float32 [16384, 2048], P('ctx', 'head')
- grad_keys: float32 [16384, 2048], P('ctx', 'head')
- grad_values: float32 [16384, 2048], P('ctx', 'head')
- grad_targets: float32 [16384, 512], P('ctx', 'head')
- grad_readout: float32 [512, 4096], P('ctx', 'head')
Inputs may be any that keep to these rules, and one draw needn't show every extreme that they name: The 128 positions of a segment are distinct, ascending, and include 0 and 511.
All inputs are finite; a program needn't handle non-finite values.
Results may differ from a plain program's by a relative error of at most 0.0081.
Values may be sent and summed in bfloat16 or wider, within the bound.
A program may use at most 192 MiB of HBM per device.

v0:
```python
from functools import reduce
import jax
import jax.numpy as jnp
from jax import lax
from jax.sharding import PartitionSpec as P

masked_score = -1e30
highest = lax.Precision.HIGHEST


def entering(value, axis, join, neutral, backward):
    count, mine = (lax.axis_size(axis), lax.axis_index(axis))
    pieces = jax.tree.map(lambda part: lax.all_gather(part, axis), value)
    if backward:
        pieces = jax.tree.map(lambda part: part[::-1], pieces)
        mine = count - 1 - mine
    subtotal = jax.tree.map(
        lambda part, zero: jnp.full_like(part, 0) + jnp.asarray(zero, part.dtype), value, neutral
    )

    def turn(position, subtotal):
        longer = join(subtotal, jax.tree.map(lambda part: part[position], pieces))
        return jax.tree.map(lambda new, old: jnp.where(position < mine, new, old), longer, subtotal)

    return lax.fori_loop(0, count - 1, turn, subtotal)


def shifted_2(value, axis, steps):
    count = lax.axis_size(axis)
    leading, last = (max(0, -steps), min(count, count - steps))
    return lax.ppermute(value, axis, [(source, source + steps) for source in range(leading, last)])


def compose(earlier_map, later_map):
    linear_part = jnp.einsum("hab,hbc->hac", later_map[0], earlier_map[0], precision=highest)
    shift_part = (
        jnp.einsum("hab,hbf->haf", later_map[0], earlier_map[1], precision=highest) + later_map[1]
    )
    return (linear_part, shift_part)


def score_block(left_rows, right_rows, score_scale):
    return (
        lax.dot_general(
            left_rows, right_rows, (((1,), (1,)), ((), ())), preferred_element_type=jnp.float32
        )
        * score_scale
    )


def gated_scores(left_rows, right_rows, usable, score_scale):
    return jnp.where(usable, score_block(left_rows, right_rows, score_scale), masked_score)


def scores_grad(cotangent, values_tile, probs_tile, row_delta):
    grad_probs = lax.dot_general(
        cotangent, values_tile, (((1,), (1,)), ((), ())), preferred_element_type=jnp.float32
    )
    return (probs_tile * (grad_probs - row_delta)).astype(jnp.bfloat16)


def block_all(
    queries_tile, cotangent, keys_tile, values_tile, probs_tile, probs_low, row_delta, score_scale
):
    grad_scores = scores_grad(cotangent, values_tile, probs_tile, row_delta)
    grad_rows = jnp.dot(grad_scores, keys_tile, preferred_element_type=jnp.float32) * score_scale
    grad_cols = (
        lax.dot_general(
            grad_scores, queries_tile, (((0,), (0,)), ((), ())), preferred_element_type=jnp.float32
        )
        * score_scale
    )
    grad_vals = lax.dot_general(
        probs_low, cotangent, (((0,), (0,)), ((), ())), preferred_element_type=jnp.float32
    )
    return (grad_rows, grad_cols, grad_vals)


def far_all(
    queries_tile, cotangent, keys_tile, values_tile, probs_tile, probs_low, row_delta, score_scale
):
    return block_all(
        queries_tile,
        cotangent,
        keys_tile,
        values_tile,
        probs_tile,
        probs_low,
        row_delta,
        score_scale,
    )


def on_device(
    queries,
    key_rows,
    value_rows,
    targets,
    readout,
    retain,
    learn_rate,
    allowed,
    positions,
    grad_out,
):
    seg_len = queries.shape[0]
    local_heads = retain.shape[1]
    head_width = queries.shape[1] // local_heads
    mem_rows = positions.shape[1]
    block_reach = allowed.shape[1]
    segment = lax.axis_index("ctx")
    score_scale = head_width ** (-0.5)
    key_heads = key_rows.reshape(seg_len, local_heads, head_width)
    key_gram = jnp.einsum("sha,shb->hab", key_heads, key_heads, preferred_element_type=jnp.float32)
    identity_block = jnp.eye(head_width, dtype=jnp.float32)
    decay_map = (
        retain[0][:, None, None] * identity_block
        - (learn_rate[0] / seg_len)[:, None, None] * key_gram
    )
    write_map = (
        jnp.einsum("sha,sf->haf", key_heads, targets, preferred_element_type=jnp.float32) / seg_len
    )
    neutral = (jnp.broadcast_to(identity_block, decay_map.shape), jnp.zeros_like(write_map))
    memory_in = entering((decay_map, write_map), "ctx", compose, neutral, False)[1]
    pick_rows = positions[0]
    picked = (
        jnp.take(queries, pick_rows, axis=0)
        .astype(jnp.float32)
        .reshape(mem_rows, local_heads, head_width)
    )
    partial_read = jnp.einsum("nha,haf->nf", picked, memory_in, precision=highest)
    hidden_read = lax.psum(partial_read, "head").astype(jnp.bfloat16)
    memory_tokens = jnp.dot(hidden_read, readout, preferred_element_type=jnp.float32).reshape(
        mem_rows, local_heads, 2, head_width
    )
    memory_keys = memory_tokens[:, :, 0].astype(jnp.bfloat16)
    memory_values = memory_tokens[:, :, 1].astype(jnp.bfloat16)
    remote = []
    for offset in range(1, block_reach + 1):
        shifted = shifted_2((key_rows, value_rows), "ctx", offset)
        usable = (allowed[segment, offset - 1] == 1) & (segment >= offset)
        remote.append((shifted[0], shifted[1], usable))
    causal = lax.broadcasted_iota(jnp.int32, (seg_len, seg_len), 0) >= lax.broadcasted_iota(
        jnp.int32, (seg_len, seg_len), 1
    )
    rows_list, keys_own, values_own = ([], [], [])
    mem_key_grads, mem_value_grads = ([], [])
    far_keys = [[] for offset in range(block_reach)]
    far_values = [[] for offset in range(block_reach)]
    max_list, total_list, delta_list = ([], [], [])
    for head_index in range(local_heads):
        columns = slice(head_index * head_width, (head_index + 1) * head_width)
        queries_tile = queries[:, columns]
        cotangent = grad_out[:, columns]
        key_collection = [memory_keys[:, head_index], key_rows[:, columns]] + [
            remote_item[0][:, columns] for remote_item in remote
        ]
        values_list = [memory_values[:, head_index], value_rows[:, columns]] + [
            remote_item[1][:, columns] for remote_item in remote
        ]
        score_list = [
            score_block(queries_tile, key_collection[0], score_scale),
            jnp.where(
                causal, score_block(queries_tile, key_collection[1], score_scale), masked_score
            ),
        ]
        score_list = score_list + [
            gated_scores(
                queries_tile, key_collection[2 + tile_index], remote[tile_index][2], score_scale
            )
            for tile_index in range(block_reach)
        ]
        row_max = reduce(
            jnp.maximum, [jnp.max(score_tile, axis=1, keepdims=True) for score_tile in score_list]
        )
        exp_tiles = [jnp.exp(score_tile - row_max) for score_tile in score_list]
        row_total = reduce(
            jnp.add, [jnp.sum(exp_tile, axis=1, keepdims=True) for exp_tile in exp_tiles]
        )
        probs_list = [exp_tile / row_total for exp_tile in exp_tiles]
        probs_lows = [probs_tile.astype(jnp.bfloat16) for probs_tile in probs_list]
        attended = reduce(
            jnp.add,
            [
                jnp.dot(low_tile, value_tile, preferred_element_type=jnp.float32)
                for low_tile, value_tile in zip(probs_lows, values_list)
            ],
        )
        row_delta = jnp.sum(cotangent.astype(jnp.float32) * attended, axis=1, keepdims=True)
        mem_grads = block_all(
            queries_tile,
            cotangent,
            key_collection[0],
            values_list[0],
            probs_list[0],
            probs_lows[0],
            row_delta,
            score_scale,
        )
        own_grads = block_all(
            queries_tile,
            cotangent,
            key_collection[1],
            values_list[1],
            probs_list[1],
            probs_lows[1],
            row_delta,
            score_scale,
        )
        grad_rows = mem_grads[0] + own_grads[0]
        for tile_index in range(block_reach):
            far_grads = far_all(
                queries_tile,
                cotangent,
                key_collection[2 + tile_index],
                values_list[2 + tile_index],
                probs_list[2 + tile_index],
                probs_lows[2 + tile_index],
                row_delta,
                score_scale,
            )
            grad_rows = grad_rows + far_grads[0]
            far_keys[tile_index].append(far_grads[1])
            far_values[tile_index].append(far_grads[2])
        rows_list.append(grad_rows)
        keys_own.append(own_grads[1])
        values_own.append(own_grads[2])
        mem_key_grads.append(mem_grads[1])
        mem_value_grads.append(mem_grads[2])
        max_list.append(row_max)
        total_list.append(row_total)
        delta_list.append(row_delta)
    grad_queries = jnp.concatenate(rows_list, axis=1)
    key_total = jnp.concatenate(keys_own, axis=1)
    value_total = jnp.concatenate(values_own, axis=1)
    for offset in range(1, block_reach + 1):
        returned = shifted_2(
            (
                jnp.concatenate(far_keys[offset - 1], axis=1),
                jnp.concatenate(far_values[offset - 1], axis=1),
            ),
            "ctx",
            -offset,
        )
        key_total = key_total + returned[0]
        value_total = value_total + returned[1]
    grad_memory = jnp.stack(
        [jnp.stack(mem_key_grads, axis=1), jnp.stack(mem_value_grads, axis=1)], axis=2
    )
    grad_memory = grad_memory.reshape(mem_rows, local_heads * 2 * head_width).astype(jnp.bfloat16)
    readout_term = lax.dot_general(
        hidden_read, grad_memory, (((0,), (0,)), ((), ())), preferred_element_type=jnp.float32
    )
    grad_readout = lax.psum_scatter(readout_term, "ctx", scatter_dimension=0, tiled=True)
    hidden_term = lax.dot_general(
        grad_memory, readout, (((1,), (1,)), ((), ())), preferred_element_type=jnp.float32
    )
    grad_hidden = lax.psum(hidden_term, "head")
    grad_picked = jnp.einsum("nf,haf->nha", grad_hidden, memory_in, precision=highest).reshape(
        mem_rows, local_heads * head_width
    )
    grad_state = jnp.einsum("nha,nf->haf", picked, grad_hidden, precision=highest)
    grad_queries = grad_queries + jnp.zeros_like(grad_queries).at[pick_rows].add(grad_picked)
    flipped = jnp.swapaxes(decay_map, 1, 2)
    grad_after = entering((flipped, grad_state), "ctx", compose, neutral, True)[1]
    grad_decay = jnp.einsum("haf,hbf->hab", grad_after, memory_in, precision=highest)
    symmetric = grad_decay + jnp.swapaxes(grad_decay, 1, 2)
    keys_wide = key_heads.astype(jnp.float32)
    key_memory = (
        jnp.einsum("sf,haf->sha", targets.astype(jnp.float32), grad_after, precision=highest)
        / seg_len
    )
    key_memory = key_memory - (learn_rate[0] / seg_len)[None, :, None] * jnp.einsum(
        "sha,hab->shb", keys_wide, symmetric, precision=highest
    )
    key_total = key_total + key_memory.reshape(seg_len, local_heads * head_width)
    target_term = jnp.einsum("sha,haf->sf", keys_wide, grad_after, precision=highest) / seg_len
    grad_targets = lax.psum_scatter(target_term, "head", scatter_dimension=1, tiled=True)
    return (grad_queries, key_total, value_total, grad_targets, grad_readout)


def solution(mesh):
    return jax.shard_map(
        on_device,
        mesh=mesh,
        in_specs=(
            P("ctx", "head"),
            P("ctx", "head"),
            P("ctx", "head"),
            P("ctx", None),
            P(None, "head"),
            P("ctx", "head"),
            P("ctx", "head"),
            P(),
            P("ctx", None),
            P("ctx", "head"),
        ),
        out_specs=(
            P("ctx", "head"),
            P("ctx", "head"),
            P("ctx", "head"),
            P("ctx", "head"),
            P("ctx", "head"),
        ),
        check_vma=False,
    )
```

profile of v0, /device:TPU:0, one launch (start us, length us, event | category | flops | bytes accessed | tf_op | source)
XLA Modules:
  0.0 802.2 jit_solution(9045116034539921850)
XLA Ops:
  15.3 2.5 convolution_multiply_fusion.14
  17.8 4.3 collective-permute-start.3
  24.4 3.1 collective-permute-start.1
  27.5 3.7 collective-permute-start
  45.8 2.7 fusion.313
  48.5 2.7 fusion.317
  51.3 2.7 fusion.311
  60.6 2.8 fusion.310
  63.4 2.8 fusion.314
  66.2 2.7 fusion.318
  68.9 2.7 fusion.322
  71.6 21.3 %all-gather.9.cloned.1.call-done = f32[128,128,128]{2,1,0:T(8,128)} async-done(((f32[4,128,128]{2,1,0:T(8,128)}), f32[128,128,128]{2,1,0:T(8,128)}) %all-gather.9.cloned.1.call-update) | async-done | bytes 8388624 | tf_op jit(solution)/shard_map/all_gather | solution.py:13
  92.9 115.6 %all-gather.11.cloned.1.call-done = f32[128,128,512]{2,1,0:T(8,128)} async-done(((f32[4,128,512]{2,1,0:T(8,128)}), f32[128,128,512]{2,1,0:T(8,128)}) %all-gather.11.cloned.1.call-update) | async-done | bytes 33554448 | tf_op jit(solution)/shard_map/all_gather | solution.py:13
  208.5 78.0 %while.28 = (s32[]{:T(128)}, f32[4,128,512]{2,1,0:T(8,128)S(1)}, s32[]{:T(128)}, f32[32,4,128,128]{3,2,1,0:T(8,128)}, f32[32,4,128,512]{3,2,1,0:T(8,128)}, /*index=5*/s32[]{:T(128)}, s32[]{:T(128)}) while((s32[]{:T(128)}, f32[4,128,512]{2,1,0:T(8,128)S(1)}, s32[]{:T(128)}, f32[32,4,128,128]{3,2,1,0:T(8,128)}, ...), condition=%wide.region_1.2_spmd.clone, body=%wide.region_0.1_spmd.clone.sunk | while | flops 403701760 | bytes 6556263 | solution.py:25
  287.8 21.1 %all-reduce.4 = bf16[128,512]{1,0:T(8,128)(2,1)S(1)} all-reduce(f32[128,512]{1,0:T(8,128)} %convolution_bitcast_fusion.1), channel_id=1, replica_groups=mesh['ctx'=32,'head'=4] {'head'}, use_global_device_ids=true, to_apply=%region_2.3 | all-reduce | flops 65536 | bytes 393216 | tf_op jit(solution)/shard_map/psum | solution.py:132
  313.8 2.4 fusion.105
  341.4 37.8 %all-reduce.3.cloned.1.call-done = f32[128,512]{1,0:T(8,128)} async-done(((f32[128,512]{1,0:T(8,128)}), f32[128,512]{1,0:T(8,128)}) %all-reduce.3.cloned.1.call-update) | async-done | bytes 262160 | tf_op jit(solution)/shard_map/psum | solution.py:258
  379.1 2.6 fusion.142
  382.3 52.2 %all-gather.13.cloned.1.call-done = f32[128,128,128]{2,1,0:T(8,128)} async-done(((f32[4,128,128]{2,1,0:T(8,128)}), f32[128,128,128]{2,1,0:T(8,128)}) %all-gather.13.cloned.1.call-update) | async-done | bytes 8388624 | tf_op jit(solution)/shard_map/all_gather | solution.py:13
  434.6 7.9 rev.6
  474.5 2.5 copy.111
  496.5 84.6 %all-gather.15.cloned.1.call-done = f32[128,128,512]{2,1,0:T(8,128)} async-done(((f32[4,128,512]{2,1,0:T(8,128)}), f32[128,128,512]{2,1,0:T(8,128)}) %all-gather.15.cloned.1.call-update) | async-done | bytes 33554448 | tf_op jit(solution)/shard_map/all_gather | solution.py:13
  581.2 23.4 %rev.7 = f32[32,4,128,512]{3,2,1,0:T(8,128)} reverse(f32[32,4,128,512]{3,2,1,0:T(8,128)} %bitcast.227), dimensions={0} | reverse | bytes 67108864 | tf_op jit(solution)/shard_map/rev | solution.py:15
  604.6 78.1 %while.29 = (s32[]{:T(128)}, f32[4,128,512]{2,1,0:T(8,128)S(1)}, s32[]{:T(128)}, f32[32,4,128,128]{3,2,1,0:T(8,128)}, f32[32,4,128,512]{3,2,1,0:T(8,128)}, /*index=5*/s32[]{:T(128)}, s32[]{:T(128)}) while((s32[]{:T(128)}, f32[4,128,512]{2,1,0:T(8,128)S(1)}, s32[]{:T(128)}, f32[32,4,128,128]{3,2,1,0:T(8,128)}, ...), condition=%wide.region_42.43_spmd.clone, body=%wide.region_41.42_spmd.clone.sunk | while | flops 403701760 | bytes 6556263 | solution.py:25
  607.2 2.4 fusion.421
  612.2 2.4 fusion.421
  682.8 4.0 fusion.42
  721.2 3.7 scatter_fusion
  724.9 3.1 fusion.97
  728.0 2.6 copy.120
  736.5 3.5 collective-permute-done.5
  745.4 49.8 %reduce-scatter.5.cloned.1.call-done = f32[16,1024]{1,0:T(8,128)} async-done(((f32[512,1024]{1,0:T(8,128)}), f32[16,1024]{1,0:T(8,128)}) %reduce-scatter.5.cloned.1.call-update) | async-done | bytes 65552 | tf_op jit(solution)/shard_map/reduce_scatter | solution.py:254
  (514 shorter events, 306.4 us)
Async XLA Ops:
  7.2 301.8 %copy-start = (bf16[512,1024]{1,0:T(8,128)(2,1)S(1)}, bf16[512,1024]{1,0:T(8,128)(2,1)}, u32[]{:S(2)}) copy-start(bf16[512,1024]{1,0:T(8,128)(2,1)} %param.18) | copy-start | bytes 3145732
  7.2 26.2 %copy-start.8 = (bf16[512,512]{1,0:T(8,128)(2,1)S(1)}, bf16[512,512]{1,0:T(8,128)(2,1)}, u32[]{:S(2)}) copy-start(bf16[512,512]{1,0:T(8,128)(2,1)} %param.15) | copy-start | bytes 1572868
  7.2 25.3 %copy-start.5 = (bf16[512,512]{1,0:T(8,128)(2,1)S(1)}, bf16[512,512]{1,0:T(8,128)(2,1)}, u32[]{:S(2)}) copy-start(bf16[512,512]{1,0:T(8,128)(2,1)} %param.23) | copy-start | bytes 1572868
  7.2 26.1 %copy-start.2 = (bf16[512,512]{1,0:T(8,128)(2,1)S(1)}, bf16[512,512]{1,0:T(8,128)(2,1)}, u32[]{:S(2)}) copy-start(bf16[512,512]{1,0:T(8,128)(2,1)} %param.14) | copy-start | bytes 1572868
  7.2 29.9 %copy-start.102 = (s32[32,2]{0,1:T(2,128)S(1)}, s32[32,2]{0,1:T(2,128)}, u32[]{:S(2)}) copy-start(s32[32,2]{0,1:T(2,128)} %param.21) | copy-start | bytes 772
  7.2 85.7 %all-gather.9.cloned.1.call-start = ((), (), s32[]{:S(2)}) async-start(), calls=%async_computation.5 | async-start | bytes 8650752 | tf_op jit(solution)/shard_map/all_gather | solution.py:13
  8.1 23.1 %copy-start.100 = (f32[4]{0:T(128)}, f32[4]{0:T(128)S(1)}, u32[]{:S(2)}) copy-start(f32[4]{0:T(128)S(1)} %multiply_bitcast_fusion) | copy-start | bytes 52
  15.2 193.2 %all-gather.11.cloned.1.call-start = ((), (), s32[]{:S(2)}) async-start(), calls=%async_computation.6 | async-start | bytes 34603008 | tf_op jit(solution)/shard_map/all_gather | solution.py:13
  17.8 361.3 %all-reduce.3.cloned.1.call-start = ((), (), s32[]{:S(2)}) async-start(), calls=%async_computation.2 | async-start | bytes 524288 | tf_op jit(solution)/shard_map/psum | solution.py:258
  17.8 305.4 %collective-permute-start.3 = (bf16[512,512]{1,0:T(8,128)(2,1)}, bf16[512,512]{1,0:T(8,128)(2,1)}, u32[]{:S(2)}, u32[]{:S(2)}) collective-permute-start(bf16[512,512]{1,0:T(8,128)(2,1)} %param.16), channel_id=1, source_target_pairs={{0,8},{4,12},{8,16},{12,20},{16,24},{20,28},{24,32},{28,36},{32,40... | collective-permute-start | bytes 1572872 | tf_op jit(solution)/shard_map/ppermute | solution.py:31
  22.2 303.4 %collective-permute-start.2 = (bf16[512,512]{1,0:T(8,128)(2,1)}, bf16[512,512]{1,0:T(8,128)(2,1)}, u32[]{:S(2)}, u32[]{:S(2)}) collective-permute-start(bf16[512,512]{1,0:T(8,128)(2,1)} %param.16), channel_id=1, source_target_pairs={{0,4},{4,8},{8,12},{12,16},{16,20},{20,24},{24,28},{28,32},{32,36}... | collective-permute-start | bytes 1572872 | tf_op jit(solution)/shard_map/ppermute | solution.py:31
  24.4 36.2 %collective-permute-start.1 = (bf16[512,512]{1,0:T(8,128)(2,1)}, bf16[512,512]{1,0:T(8,128)(2,1)}, u32[]{:S(2)}, u32[]{:S(2)}) collective-permute-start(bf16[512,512]{1,0:T(8,128)(2,1)} %param.15), channel_id=1, source_target_pairs={{0,8},{4,12},{8,16},{12,20},{16,24},{20,28},{24,32},{28,36},{32,40... | collective-permute-start | bytes 1572872 | tf_op jit(solution)/shard_map/ppermute | solution.py:31
  27.5 23.8 %collective-permute-start = (bf16[512,512]{1,0:T(8,128)(2,1)}, bf16[512,512]{1,0:T(8,128)(2,1)}, u32[]{:S(2)}, u32[]{:S(2)}) collective-permute-start(bf16[512,512]{1,0:T(8,128)(2,1)} %param.15), channel_id=1, source_target_pairs={{0,4},{4,8},{8,12},{12,16},{16,20},{20,24},{24,28},{28,32},{32,36}... | collective-permute-start | bytes 1572872 | tf_op jit(solution)/shard_map/ppermute | solution.py:31
  32.5 254.0 %copy-start.96 = (pred[128]{0:T(512)(128)(4,1)}, pred[128]{0:T(512)(128)(4,1)S(1)}, u32[]{:S(2)}) copy-start(pred[128]{0:T(512)(128)(4,1)S(1)} %compare_and_fusion) | copy-start | bytes 388
  40.0 246.6 %copy-start.63 = (bf16[128,512]{0,1:T(8,128)(2,1)}, bf16[128,512]{0,1:T(8,128)(2,1)S(1)}, u32[]{:S(2)}) copy-start(bf16[128,512]{0,1:T(8,128)(2,1)S(1)} %copy.137) | copy-start | bytes 393220
  316.2 21.0 %copy-start.78 = (f32[512]{0:T(512)}, f32[512]{0:T(512)S(1)}, u32[]{:S(2)}) copy-start(f32[512]{0:T(512)S(1)} %add_add_fusion.2) | copy-start | bytes 6148
  318.0 15.5 %copy-start.80 = (f32[512]{0:T(512)}, f32[512]{0:T(512)S(1)}, u32[]{:S(2)}) copy-start(f32[512]{0:T(512)S(1)} %add_add_fusion.3) | copy-start | bytes 6148
  339.5 95.1 %all-gather.13.cloned.1.call-start = ((), (), s32[]{:S(2)}) async-start(), calls=%async_computation.7 | async-start | bytes 8650752 | tf_op jit(solution)/shard_map/all_gather | solution.py:13
  341.3 239.8 %all-gather.15.cloned.1.call-start = ((), (), s32[]{:S(2)}) async-start(), calls=%async_computation.8 | async-start | bytes 34603008 | tf_op jit(solution)/shard_map/all_gather | solution.py:13
  381.7 361.8 %reduce-scatter.3.cloned.1.call-start = ((), (), s32[]{:S(2)}) async-start(), calls=%async_computation.3 | async-start | bytes 1310720 | tf_op jit(solution)/shard_map/reduce_scatter | solution.py:278
  477.1 16.4 %copy-start.27 = (bf16[512,512]{0,1:T(8,128)(2,1)S(1)}, bf16[512,512]{0,1:T(8,128)(2,1)}, u32[]{:S(2)}) copy-start(bf16[512,512]{0,1:T(8,128)(2,1)} %copy-done.26) | copy-start | bytes 1572868
  477.1 17.5 %copy-start.29 = (bf16[512,512]{0,1:T(8,128)(2,1)S(1)}, bf16[512,512]{0,1:T(8,128)(2,1)}, u32[]{:S(2)}) copy-start(bf16[512,512]{0,1:T(8,128)(2,1)} %copy-done.28) | copy-start | bytes 1572868
  477.1 18.5 %copy-start.31 = (bf16[512,512]{0,1:T(8,128)(2,1)S(1)}, bf16[512,512]{0,1:T(8,128)(2,1)}, u32[]{:S(2)}) copy-start(bf16[512,512]{0,1:T(8,128)(2,1)} %copy-done.30) | copy-start | bytes 1572868
  484.2 252.3 %collective-permute-start.4 = (f32[512,512]{0,1:T(8,128)}, f32[512,512]{0,1:T(8,128)}, u32[]{:S(2)}, u32[]{:S(2)}) collective-permute-start(f32[512,512]{0,1:T(8,128)} %pad_maximum_fusion.1), channel_id=1, source_target_pairs={{4,0},{8,4},{12,8},{16,12},{20,16},{24,20},{28,24},{32,28},{36,32}... | collective-permute-start | bytes 3145736 | tf_op jit(solution)/shard_map/ppermute | solution.py:31
  491.0 233.9 %collective-permute-start.7 = (f32[512,512]{0,1:T(8,128)}, f32[512,512]{0,1:T(8,128)}, u32[]{:S(2)}, u32[]{:S(2)}) collective-permute-start(f32[512,512]{0,1:T(8,128)} %pad_maximum_fusion.4), channel_id=1, source_target_pairs={{8,0},{12,4},{16,8},{20,12},{24,16},{28,20},{32,24},{36,28},{40,32... | collective-permute-start | bytes 3145736 | tf_op jit(solution)/shard_map/ppermute | solution.py:31
  682.7 16.0 %copy-start.4 = (bf16[512,512]{1,0:T(8,128)(2,1)S(1)}, bf16[512,512]{1,0:T(8,128)(2,1)}, u32[]{:S(2)}) copy-start(bf16[512,512]{1,0:T(8,128)(2,1)} %param.14) | copy-start | bytes 1572868
  686.7 108.4 %reduce-scatter.5.cloned.1.call-start = ((), (), s32[]{:S(2)}) async-start(), calls=%async_computation.4 | async-start | bytes 2162688 | tf_op jit(solution)/shard_map/reduce_scatter | solution.py:254
  689.1 35.8 %collective-permute-start.6 = (f32[512,512]{0,1:T(8,128)}, f32[512,512]{0,1:T(8,128)}, u32[]{:S(2)}, u32[]{:S(2)}) collective-permute-start(f32[512,512]{0,1:T(8,128)} %pad_maximum_fusion.3), channel_id=1, source_target_pairs={{4,0},{8,4},{12,8},{16,12},{20,16},{24,20},{28,24},{32,28},{36,32}... | collective-permute-start | bytes 3145736 | tf_op jit(solution)/shard_map/ppermute | solution.py:31
  696.7 24.5 %copy-start.98 = (s32[128]{0:T(128)S(1)}, s32[128]{0:T(128)}, u32[]{:S(2)}) copy-start(s32[128]{0:T(128)} %copy-done.97) | copy-start | bytes 1540
  706.8 18.1 %copy-start.64 = (f32[512,128]{0,1:T(8,128)S(1)}, f32[512,128]{0,1:T(8,128)}, u32[]{:S(2)}) copy-start(f32[512,128]{0,1:T(8,128)} %fusion.279) | copy-start | bytes 786436
  711.6 28.4 %collective-permute-start.5 = (f32[512,512]{0,1:T(8,128)}, f32[512,512]{0,1:T(8,128)}, u32[]{:S(2)}, u32[]{:S(2)}) collective-permute-start(f32[512,512]{0,1:T(8,128)} %pad_maximum_fusion.2), channel_id=1, source_target_pairs={{8,0},{12,4},{16,8},{20,12},{24,16},{28,20},{32,24},{36,28},{40,32... | collective-permute-start | bytes 3145736 | tf_op jit(solution)/shard_map/ppermute | solution.py:31
  728.0 67.1 %copy-start.1 = (bf16[512,1024]{1,0:T(8,128)(2,1)S(1)}, bf16[512,1024]{1,0:T(8,128)(2,1)}, u32[]{:S(2)}) copy-start(bf16[512,1024]{1,0:T(8,128)(2,1)} %param.18) | copy-start | bytes 3145732
  (86 other events, 599.6 us)
Sparse Core Ops, SparseCore 0:
  15.4 77.4 all-gather.8
  95.1 113.3 all-gather.10
  339.6 39.4 all-reduce.2
  381.2 53.2 all-gather.12
  436.7 144.4 all-gather.14
  686.9 25.3 reduce-scatter.2
  716.3 78.7 reduce-scatter.4
where the time goes:
time: 812 us; the launch traced here: 802 us
  waiting for transfers between devices  365 us (45%)
  matrix products  281 us (35%)
  local copies, waits for them, and re-layouts  66.5 us (8%)
  other arithmetic  29.6 us (4%)
  blocking collectives  21.1 us (3%)
  starting transfers between devices  19.5 us (2%)
  between operations  17.7 us (2%)
    all_gather x4, waiting for transfers between devices, entering(): pieces = jax.tree.map(lambda part: lax.all_gather(part, axis), value)  274 us
    dot_general x62, matrix products, compose(): jnp.einsum('hab,hbf->haf', later_map[0], earlier_map[1], precision=highest)  150 us
    reduce_scatter x1, waiting for transfers between devices, on_device(): lax.psum_scatter(readout_term, 'ctx', scatter_dimension=0, tiled=True)  49.8 us
    psum x1, waiting for transfers between devices, on_device(): grad_hidden = lax.psum(hidden_term, 'head')  37.8 us
    rev x2, local copies, waits for them, and re-layouts, entering(): pieces = jax.tree.map(lambda part: part[::-1], pieces)  31.3 us
    dot_general x16, matrix products, score_block(): lax.dot_general(left_rows, right_rows, (((1,), (1,)), ((), ())), preferre...  30.4 us
    dot_general x16, matrix products, block_all(): lax.dot_general(grad_scores, queries_tile, (((0,), (0,)), ((), ())), pref...  22.2 us
    psum x1, blocking collectives, on_device(): hidden_read = lax.psum(partial_read, 'head').astype(jnp.bfloat16)  21.1 us
  transfers between devices with their start and end apart: 15, of which 7 were waited for; matrix products, arithmetic and copies ran while one was open for 44% of the time, Pallas kernels for 0%

commit v1 on v0

--- a/solution.py
+++ b/solution.py
@@ -255,7 +255,11 @@
     hidden_term = lax.dot_general(
         grad_memory, readout, (((1,), (1,)), ((), ())), preferred_element_type=jnp.float32
     )
-    grad_hidden = lax.psum(hidden_term, "head")
+    grad_hidden = hidden_term
+    for hop in (1, 2):
+        grad_hidden = grad_hidden + lax.ppermute(
+            grad_hidden, "head", [(dev, dev ^ hop) for dev in range(4)]
+        )
     grad_picked = jnp.einsum("nf,haf->nha", grad_hidden, memory_in, precision=highest).reshape(
         mem_rows, local_heads * head_width
     )

time: 812 us -> 732 us (0.901)
  waiting for transfers between devices: 365 us -> 285 us
    all_gather x4, waiting for transfers between devices: 274 us -> 215 us  [entering(): pieces = jax.tree.map(lambda part: lax.all_gather(part, axis), value)]
    psum x1 -> x0, waiting for transfers between devices: 37.8 us -> none  [on_device(): grad_hidden = lax.psum(hidden_term, 'head')]
    ppermute x0 -> x2, waiting for transfers between devices: none -> 16.7 us  [on_device(): lax.ppermute(grad_hidden, 'head', [(dev, dev ^ hop) for dev in range(4)])]
    unnamed x216 -> x220, local copies, waits for them, and re-layouts: 18.7 us -> 18.9 us
  transfers between devices with their start and end apart: 15 -> 16, of which waited for: 7 -> 7; matrix products, arithmetic and copies ran while one was open for 44% -> 50% of each run, Pallas kernels for 0% -> 0%
where the time goes in v1:
time: 732 us; the launch traced here: 722 us
  waiting for transfers between devices  285 us (39%)
  matrix products  279 us (38%)
  local copies, waits for them, and re-layouts  67.3 us (9%)
  other arithmetic  29.4 us (4%)
  blocking collectives  21.1 us (3%)
  starting transfers between devices  19.8 us (3%)
  between operations  17.9 us (2%)
    all_gather x4, waiting for transfers between devices, entering(): pieces = jax.tree.map(lambda part: lax.all_gather(part, axis), value)  215 us
    dot_general x62, matrix products, compose(): jnp.einsum('hab,hbf->haf', later_map[0], earlier_map[1], precision=highest)  150 us
    reduce_scatter x1, waiting for transfers between devices, on_device(): lax.psum_scatter(readout_term, 'ctx', scatter_dimension=0, tiled=True)  49.7 us
    rev x2, local copies, waits for them, and re-layouts, entering(): pieces = jax.tree.map(lambda part: part[::-1], pieces)  31.8 us
    dot_general x16, matrix products, score_block(): lax.dot_general(left_rows, right_rows, (((1,), (1,)), ((), ())), preferre...  30.5 us
    dot_general x16, matrix products, block_all(): lax.dot_general(grad_scores, queries_tile, (((0,), (0,)), ((), ())), pref...  21.7 us
    psum x1, blocking collectives, on_device(): hidden_read = lax.psum(partial_read, 'head').astype(jnp.bfloat16)  21.1 us
    unnamed x220, local copies, waits for them, and re-layouts  18.9 us
  transfers between devices with their start and end apart: 16, of which 7 were waited for; matrix products, arithmetic and copies ran while one was open for 50% of the time, Pallas kernels for 0%

profile of v1, /device:TPU:0, one launch (start us, length us, event | category | flops | bytes accessed | tf_op | source)
XLA Modules:
  0.0 722.2 jit_solution(18244252271917710028)
XLA Ops:
  15.3 2.5 convolution_multiply_fusion.14
  17.8 4.3 collective-permute-start.3
  24.4 3.1 collective-permute-start.1
  27.5 3.7 collective-permute-start
  46.4 2.7 fusion.315
  49.1 2.8 fusion.319
  54.1 2.8 fusion.317
  61.3 2.8 fusion.312
  64.0 2.8 fusion.316
  66.8 2.7 fusion.320
  69.6 2.8 fusion.324
  72.3 20.5 %all-gather.9.cloned.1.call-done = f32[128,128,128]{2,1,0:T(8,128)} async-done(((f32[4,128,128]{2,1,0:T(8,128)}), f32[128,128,128]{2,1,0:T(8,128)}) %all-gather.9.cloned.1.call-update) | async-done | bytes 8388624 | tf_op jit(solution)/shard_map/all_gather | solution.py:13
  92.8 115.6 %all-gather.11.cloned.1.call-done = f32[128,128,512]{2,1,0:T(8,128)} async-done(((f32[4,128,512]{2,1,0:T(8,128)}), f32[128,128,512]{2,1,0:T(8,128)}) %all-gather.11.cloned.1.call-update) | async-done | bytes 33554448 | tf_op jit(solution)/shard_map/all_gather | solution.py:13
  208.5 78.4 %while.28 = (s32[]{:T(128)}, f32[4,128,512]{2,1,0:T(8,128)S(1)}, s32[]{:T(128)}, f32[32,4,128,128]{3,2,1,0:T(8,128)}, f32[32,4,128,512]{3,2,1,0:T(8,128)}, /*index=5*/s32[]{:T(128)}, s32[]{:T(128)}) while((s32[]{:T(128)}, f32[4,128,512]{2,1,0:T(8,128)S(1)}, s32[]{:T(128)}, f32[32,4,128,128]{3,2,1,0:T(8,128)}, ...), condition=%wide.region_1.2_spmd.clone, body=%wide.region_0.1_spmd.clone.sunk | while | flops 403701760 | bytes 6556263 | solution.py:25
  218.6 2.5 fusion.420
  246.4 2.5 fusion.420
  249.0 2.5 fusion.420
  251.6 2.5 fusion.420
  288.2 21.1 %all-reduce.1 = bf16[128,512]{1,0:T(8,128)(2,1)S(1)} all-reduce(f32[128,512]{1,0:T(8,128)} %convolution_bitcast_fusion.1), channel_id=1, replica_groups=mesh['ctx'=32,'head'=4] {'head'}, use_global_device_ids=true, to_apply=%region_2.3 | all-reduce | flops 65536 | bytes 393216 | tf_op jit(solution)/shard_map/psum | solution.py:132
  340.7 9.1 %collective-permute-done.4 = f32[128,512]{1,0:T(8,128)S(1)} collective-permute-done((f32[128,512]{1,0:T(8,128)S(1)}, f32[128,512]{1,0:T(8,128)S(1)}, u32[]{:S(2)}, u32[]{:S(2)}) %collective-permute-start.4) | collective-permute-done | bytes 262176 | tf_op jit(solution)/shard_map/ppermute | solution.py:260
  350.1 7.7 %collective-permute-done.5 = f32[128,512]{1,0:T(8,128)S(1)} collective-permute-done((f32[128,512]{1,0:T(8,128)S(1)}, f32[128,512]{1,0:T(8,128)S(1)}, u32[]{:S(2)}, u32[]{:S(2)}) %collective-permute-start.5) | collective-permute-done | bytes 262176 | tf_op jit(solution)/shard_map/ppermute | solution.py:260
  360.1 8.4 %rev.6 = f32[32,4,128,128]{3,2,1,0:T(8,128)} reverse(f32[32,4,128,128]{3,2,1,0:T(8,128)} %bitcast.228), dimensions={0} | reverse | bytes 16777216 | tf_op jit(solution)/shard_map/rev | solution.py:15
  400.6 2.5 copy.111
  422.2 79.2 %all-gather.15.cloned.1.call-done = f32[128,128,512]{2,1,0:T(8,128)} async-done(((f32[4,128,512]{2,1,0:T(8,128)}), f32[128,128,512]{2,1,0:T(8,128)}) %all-gather.15.cloned.1.call-update) | async-done | bytes 33554448 | tf_op jit(solution)/shard_map/all_gather | solution.py:13
  501.3 23.4 %rev.7 = f32[32,4,128,512]{3,2,1,0:T(8,128)} reverse(f32[32,4,128,512]{3,2,1,0:T(8,128)} %bitcast.227), dimensions={0} | reverse | bytes 67108864 | tf_op jit(solution)/shard_map/rev | solution.py:15
  524.7 78.1 %while.29 = (s32[]{:T(128)}, f32[4,128,512]{2,1,0:T(8,128)S(1)}, s32[]{:T(128)}, f32[32,4,128,128]{3,2,1,0:T(8,128)}, f32[32,4,128,512]{3,2,1,0:T(8,128)}, /*index=5*/s32[]{:T(128)}, s32[]{:T(128)}) while((s32[]{:T(128)}, f32[4,128,512]{2,1,0:T(8,128)S(1)}, s32[]{:T(128)}, f32[32,4,128,128]{3,2,1,0:T(8,128)}, ...), condition=%wide.region_41.42_spmd.clone, body=%wide.region_40.41_spmd.clone.sunk | while | flops 403701760 | bytes 6556263 | solution.py:25
  602.9 4.0 fusion.42
  641.3 3.7 scatter_fusion
  645.0 3.2 fusion.97
  648.2 2.6 copy.120
  656.7 3.4 collective-permute-done.7
  665.5 49.7 %reduce-scatter.5.cloned.1.call-done = f32[16,1024]{1,0:T(8,128)} async-done(((f32[512,1024]{1,0:T(8,128)}), f32[16,1024]{1,0:T(8,128)}) %reduce-scatter.5.cloned.1.call-update) | async-done | bytes 65552 | tf_op jit(solution)/shard_map/reduce_scatter | solution.py:254
  (520 shorter events, 305.1 us)
Async XLA Ops:
  7.2 302.1 %copy-start = (bf16[512,1024]{1,0:T(8,128)(2,1)S(1)}, bf16[512,1024]{1,0:T(8,128)(2,1)}, u32[]{:S(2)}) copy-start(bf16[512,1024]{1,0:T(8,128)(2,1)} %param.18) | copy-start | bytes 3145732
  7.2 26.0 %copy-start.8 = (bf16[512,512]{1,0:T(8,128)(2,1)S(1)}, bf16[512,512]{1,0:T(8,128)(2,1)}, u32[]{:S(2)}) copy-start(bf16[512,512]{1,0:T(8,128)(2,1)} %param.15) | copy-start | bytes 1572868
  7.2 25.9 %copy-start.104 = (s32[1,128]{1,0:T(1,128)S(1)}, s32[1,128]{1,0:T(1,128)}, u32[]{:S(2)}) copy-start(s32[1,128]{1,0:T(1,128)} %param.22) | copy-start | bytes 1540
  7.2 25.9 %copy-start.2 = (bf16[512,512]{1,0:T(8,128)(2,1)S(1)}, bf16[512,512]{1,0:T(8,128)(2,1)}, u32[]{:S(2)}) copy-start(bf16[512,512]{1,0:T(8,128)(2,1)} %param.14) | copy-start | bytes 1572868
  7.2 29.7 %copy-start.5 = (bf16[512,512]{1,0:T(8,128)(2,1)S(1)}, bf16[512,512]{1,0:T(8,128)(2,1)}, u32[]{:S(2)}) copy-start(bf16[512,512]{1,0:T(8,128)(2,1)} %param.23) | copy-start | bytes 1572868
  7.2 30.5 %copy-start.103 = (s32[32,2]{0,1:T(2,128)S(1)}, s32[32,2]{0,1:T(2,128)}, u32[]{:S(2)}) copy-start(s32[32,2]{0,1:T(2,128)} %param.21) | copy-start | bytes 772
  7.2 85.6 %all-gather.9.cloned.1.call-start = ((), (), s32[]{:S(2)}) async-start(), calls=%async_computation.4 | async-start | bytes 8650752 | tf_op jit(solution)/shard_map/all_gather | solution.py:13
  8.1 25.0 %copy-start.101 = (f32[4]{0:T(128)}, f32[4]{0:T(128)S(1)}, u32[]{:S(2)}) copy-start(f32[4]{0:T(128)S(1)} %multiply_bitcast_fusion) | copy-start | bytes 52
  15.2 193.2 %all-gather.11.cloned.1.call-start = ((), (), s32[]{:S(2)}) async-start(), calls=%async_computation.5 | async-start | bytes 34603008 | tf_op jit(solution)/shard_map/all_gather | solution.py:13
  17.8 342.3 %all-gather.13.cloned.1.call-start = ((), (), s32[]{:S(2)}) async-start(), calls=%async_computation.6 | async-start | bytes 8650752 | tf_op jit(solution)/shard_map/all_gather | solution.py:13
  17.8 304.9 %collective-permute-start.3 = (bf16[512,512]{1,0:T(8,128)(2,1)}, bf16[512,512]{1,0:T(8,128)(2,1)}, u32[]{:S(2)}, u32[]{:S(2)}) collective-permute-start(bf16[512,512]{1,0:T(8,128)(2,1)} %param.16), channel_id=1, source_target_pairs={{0,8},{4,12},{8,16},{12,20},{16,24},{20,28},{24,32},{28,36},{32,40... | collective-permute-start | bytes 1572872 | tf_op jit(solution)/shard_map/ppermute | solution.py:31
  22.1 302.2 %collective-permute-start.2 = (bf16[512,512]{1,0:T(8,128)(2,1)}, bf16[512,512]{1,0:T(8,128)(2,1)}, u32[]{:S(2)}, u32[]{:S(2)}) collective-permute-start(bf16[512,512]{1,0:T(8,128)(2,1)} %param.16), channel_id=1, source_target_pairs={{0,4},{4,8},{8,12},{12,16},{16,20},{20,24},{24,28},{28,32},{32,36}... | collective-permute-start | bytes 1572872 | tf_op jit(solution)/shard_map/ppermute | solution.py:31
  24.4 36.9 %collective-permute-start.1 = (bf16[512,512]{1,0:T(8,128)(2,1)}, bf16[512,512]{1,0:T(8,128)(2,1)}, u32[]{:S(2)}, u32[]{:S(2)}) collective-permute-start(bf16[512,512]{1,0:T(8,128)(2,1)} %param.15), channel_id=1, source_target_pairs={{0,8},{4,12},{8,16},{12,20},{16,24},{20,28},{24,32},{28,36},{32,40... | collective-permute-start | bytes 1572872 | tf_op jit(solution)/shard_map/ppermute | solution.py:31
  27.5 24.4 %collective-permute-start = (bf16[512,512]{1,0:T(8,128)(2,1)}, bf16[512,512]{1,0:T(8,128)(2,1)}, u32[]{:S(2)}, u32[]{:S(2)}) collective-permute-start(bf16[512,512]{1,0:T(8,128)(2,1)} %param.15), channel_id=1, source_target_pairs={{0,4},{4,8},{8,12},{12,16},{16,20},{20,24},{24,28},{28,32},{32,36}... | collective-permute-start | bytes 1572872 | tf_op jit(solution)/shard_map/ppermute | solution.py:31
  33.0 468.3 %all-gather.15.cloned.1.call-start = ((), (), s32[]{:S(2)}) async-start(), calls=%async_computation.7 | async-start | bytes 34603008 | tf_op jit(solution)/shard_map/all_gather | solution.py:13
  33.2 253.7 %copy-start.89 = (pred[128]{0:T(512)(128)(4,1)}, pred[128]{0:T(512)(128)(4,1)S(1)}, u32[]{:S(2)}) copy-start(pred[128]{0:T(512)(128)(4,1)S(1)} %compare_and_fusion) | copy-start | bytes 388
  40.6 246.4 %copy-start.63 = (bf16[128,512]{0,1:T(8,128)(2,1)}, bf16[128,512]{0,1:T(8,128)(2,1)S(1)}, u32[]{:S(2)}) copy-start(bf16[128,512]{0,1:T(8,128)(2,1)S(1)} %copy.137) | copy-start | bytes 393220
  319.2 20.3 %copy-start.81 = (f32[512]{0:T(512)}, f32[512]{0:T(512)S(1)}, u32[]{:S(2)}) copy-start(f32[512]{0:T(512)S(1)} %add_add_fusion.2) | copy-start | bytes 6148
  334.1 23.7 %copy-start.64 = (bf16[128,512]{0,1:T(8,128)(2,1)S(1)}, bf16[128,512]{0,1:T(8,128)(2,1)}, u32[]{:S(2)}) copy-start(bf16[128,512]{0,1:T(8,128)(2,1)} %copy-done.63) | copy-start | bytes 393220
  334.1 23.7 %copy-start.90 = (pred[128]{0:T(512)(128)(4,1)S(1)}, pred[128]{0:T(512)(128)(4,1)}, u32[]{:S(2)}) copy-start(pred[128]{0:T(512)(128)(4,1)} %copy-done.89) | copy-start | bytes 388
  335.3 22.4 %copy-start.95 = (f32[512]{0:T(512)}, f32[512]{0:T(512)S(1)}, u32[]{:S(2)}) copy-start(f32[512]{0:T(512)S(1)} %fusion.79) | copy-start | bytes 6148
  335.6 22.2 %copy-start.78 = (bf16[128,512]{1,0:T(8,128)(2,1)}, bf16[128,512]{1,0:T(8,128)(2,1)S(1)}, u32[]{:S(2)}) copy-start(bf16[128,512]{1,0:T(8,128)(2,1)S(1)} %fusion.75) | copy-start | bytes 393220
  340.6 9.2 %collective-permute-start.4 = (f32[128,512]{1,0:T(8,128)S(1)}, f32[128,512]{1,0:T(8,128)S(1)}, u32[]{:S(2)}, u32[]{:S(2)}) collective-permute-start(f32[128,512]{1,0:T(8,128)S(1)} %fusion.328), channel_id=1, source_target_pairs={{0,1},{1,0},{2,3},{3,2},{4,5},{5,4},{6,7},{7,6},{8,9},{9,8},{10,11... | collective-permute-start | bytes 786440 | tf_op jit(solution)/shard_map/ppermute | solution.py:260
  349.8 8.0 %collective-permute-start.5 = (f32[128,512]{1,0:T(8,128)S(1)}, f32[128,512]{1,0:T(8,128)S(1)}, u32[]{:S(2)}, u32[]{:S(2)}) collective-permute-start(f32[128,512]{1,0:T(8,128)S(1)} %add.328), channel_id=1, source_target_pairs={{0,2},{1,3},{2,0},{3,1},{4,6},{5,7},{6,4},{7,5},{8,10},{9,11},{10,... | collective-permute-start | bytes 786440 | tf_op jit(solution)/shard_map/ppermute | solution.py:260
  359.4 304.2 %reduce-scatter.3.cloned.1.call-start = ((), (), s32[]{:S(2)}) async-start(), calls=%async_computation.2 | async-start | bytes 1310720 | tf_op jit(solution)/shard_map/reduce_scatter | solution.py:282
  409.8 246.9 %collective-permute-start.6 = (f32[512,512]{0,1:T(8,128)}, f32[512,512]{0,1:T(8,128)}, u32[]{:S(2)}, u32[]{:S(2)}) collective-permute-start(f32[512,512]{0,1:T(8,128)} %pad_maximum_fusion.1), channel_id=1, source_target_pairs={{4,0},{8,4},{12,8},{16,12},{20,16},{24,20},{28,24},{32,28},{36,32}... | collective-permute-start | bytes 3145736 | tf_op jit(solution)/shard_map/ppermute | solution.py:31
  416.6 228.4 %collective-permute-start.9 = (f32[512,512]{0,1:T(8,128)}, f32[512,512]{0,1:T(8,128)}, u32[]{:S(2)}, u32[]{:S(2)}) collective-permute-start(f32[512,512]{0,1:T(8,128)} %pad_maximum_fusion.4), channel_id=1, source_target_pairs={{8,0},{12,4},{16,8},{20,12},{24,16},{28,20},{32,24},{36,28},{40,32... | collective-permute-start | bytes 3145736 | tf_op jit(solution)/shard_map/ppermute | solution.py:31
  606.9 108.2 %reduce-scatter.5.cloned.1.call-start = ((), (), s32[]{:S(2)}) async-start(), calls=%async_computation.3 | async-start | bytes 2162688 | tf_op jit(solution)/shard_map/reduce_scatter | solution.py:254
  609.2 35.8 %collective-permute-start.8 = (f32[512,512]{0,1:T(8,128)}, f32[512,512]{0,1:T(8,128)}, u32[]{:S(2)}, u32[]{:S(2)}) collective-permute-start(f32[512,512]{0,1:T(8,128)} %pad_maximum_fusion.3), channel_id=1, source_target_pairs={{4,0},{8,4},{12,8},{16,12},{20,16},{24,20},{28,24},{32,28},{36,32}... | collective-permute-start | bytes 3145736 | tf_op jit(solution)/shard_map/ppermute | solution.py:31
  618.9 22.5 %copy-start.100 = (s32[128]{0:T(128)S(1)}, s32[128]{0:T(128)}, u32[]{:S(2)}) copy-start(s32[128]{0:T(128)} %copy-done.99) | copy-start | bytes 1540
  631.7 28.4 %collective-permute-start.7 = (f32[512,512]{0,1:T(8,128)}, f32[512,512]{0,1:T(8,128)}, u32[]{:S(2)}, u32[]{:S(2)}) collective-permute-start(f32[512,512]{0,1:T(8,128)} %pad_maximum_fusion.2), channel_id=1, source_target_pairs={{8,0},{12,4},{16,8},{20,12},{24,16},{28,20},{32,24},{36,28},{40,32... | collective-permute-start | bytes 3145736 | tf_op jit(solution)/shard_map/ppermute | solution.py:31
  648.2 66.9 %copy-start.1 = (bf16[512,1024]{1,0:T(8,128)(2,1)S(1)}, bf16[512,1024]{1,0:T(8,128)(2,1)}, u32[]{:S(2)}) copy-start(bf16[512,1024]{1,0:T(8,128)(2,1)} %param.18) | copy-start | bytes 3145732
  (89 other events, 733.8 us)
Sparse Core Ops, SparseCore 0:
  15.3 77.4 all-gather.8
  95.1 113.3 all-gather.10
  210.7 52.0 all-gather.12
  359.6 141.7 all-gather.14
  607.0 25.2 reduce-scatter.2
  636.3 78.7 reduce-scatter.4
